TPU v7x, 32 devices: a whole 2x2x4 slice. The times are simulated.
32 devices in a mesh: pix: 16 (over z, x, core), rep: 2 (over y).
Axes of the slice: x: 2, y: 2, z: 4, core: 2. Of those that a mesh axis runs over, the one named last changes fastest.
Arguments:
- tokens: bfloat16 [256, 16, 1152], P(('pix', 'rep')), may hold values from -48 to 48
- out_grad: bfloat16 [256, 16, 1152], P(('pix', 'rep')), may hold values from -6 to 6
- query_weight: bfloat16 [1152, 1152], P('pix'), may hold values from -0.1875 to 0.1875
- key_weight: bfloat16 [1152, 1152], P('pix'), may hold values from -0.1875 to 0.1875
- value_weight: bfloat16 [1152, 1152], P('pix'), may hold values from -0.1875 to 0.1875
- output_weight: bfloat16 [1152, 1152], P('pix'), may hold values from -0.1875 to 0.1875
Outputs:
- input_grad: bfloat16 [256, 16, 1152], P(('pix', 'rep'))
- weight_grads: float32 [1152, 4608], P('pix')
All inputs are finite; a program needn't handle non-finite values.
Results may differ from a plain program's by a relative error of at most 0.025.
The roundings to bfloat16 on the way count: a program that leaves them out, or rounds other values in their place, can miss the bound.
Values may be sent and summed in bfloat16 or wider, within the bound.
No kernel may reach another device: no remote copies, remote signals or barrier semaphores. Data moves between devices by JAX's collectives and lax.ppermute only.
A program may use at most 128 MiB of HBM per device.

v0:
```python
import jax
import jax.numpy as jnp
from jax import lax
from jax.sharding import PartitionSpec as P

D = 1152
HEADS = 16
HEAD_DIM = 72
FRAMES = 16


def contract_last(left, right):
    return lax.dot_general(
        left, right, (((1,), (1,)), ((), ())), preferred_element_type=jnp.float32
    )


def contract_first(left, right):
    return lax.dot_general(
        left, right, (((0,), (0,)), ((), ())), preferred_element_type=jnp.float32
    )


def local(tokens, out_grad, query_weight, key_weight, value_weight, output_weight):
    count = tokens.shape[0]
    rows = tokens.reshape(-1, D)
    drows = out_grad.reshape(-1, D)
    scale = 1.0 / HEAD_DIM**0.5
    full_q, full_k, full_v = (
        lax.all_gather(query_weight, "pix", axis=0, tiled=True),
        lax.all_gather(key_weight, "pix", axis=0, tiled=True),
        lax.all_gather(value_weight, "pix", axis=0, tiled=True),
    )
    query = jnp.dot(rows, full_q, preferred_element_type=jnp.float32).astype(jnp.bfloat16)
    keyed = jnp.dot(rows, full_k, preferred_element_type=jnp.float32).astype(jnp.bfloat16)
    valued = jnp.dot(rows, full_v, preferred_element_type=jnp.float32).astype(jnp.bfloat16)
    shape4 = (count, FRAMES, HEADS, HEAD_DIM)
    qh = query.reshape(shape4)
    kh = keyed.reshape(shape4)
    vh = valued.reshape(shape4)
    scores = jnp.einsum("sfhe,sghe->shfg", qh, kh, preferred_element_type=jnp.float32) * scale
    scores = scores - jnp.max(scores, axis=-1, keepdims=True)
    expo = jnp.exp(scores)
    probs = expo / jnp.sum(expo, axis=-1, keepdims=True)
    probs_b = probs.astype(jnp.bfloat16)
    attended = (
        jnp.einsum("shfg,sghe->sfhe", probs_b, vh, preferred_element_type=jnp.float32)
        .reshape(-1, D)
        .astype(jnp.bfloat16)
    )
    output_full = lax.all_gather(output_weight, "pix", axis=0, tiled=True)
    dattn = contract_last(drows, output_full).astype(jnp.bfloat16)
    dah = dattn.reshape(shape4)
    dvalue = (
        jnp.einsum("shfg,sfhe->sghe", probs_b, dah, preferred_element_type=jnp.float32)
        .reshape(-1, D)
        .astype(jnp.bfloat16)
    )
    dprobs = jnp.einsum("sfhe,sghe->shfg", dah, vh, preferred_element_type=jnp.float32)
    dscore = (probs * (dprobs - jnp.sum(dprobs * probs, axis=-1, keepdims=True)) * scale).astype(
        jnp.bfloat16
    )
    dquery = (
        jnp.einsum("shfg,sghe->sfhe", dscore, kh, preferred_element_type=jnp.float32)
        .reshape(-1, D)
        .astype(jnp.bfloat16)
    )
    dkey = (
        jnp.einsum("shfg,sfhe->sghe", dscore, qh, preferred_element_type=jnp.float32)
        .reshape(-1, D)
        .astype(jnp.bfloat16)
    )
    grads = lax.psum_scatter(
        jnp.concatenate(
            [
                jnp.concatenate(
                    [
                        contract_first(rows, dquery),
                        contract_first(rows, dkey),
                        contract_first(rows, dvalue),
                    ],
                    axis=1,
                ),
                contract_first(attended, drows),
            ],
            axis=1,
        ).astype(jnp.bfloat16),
        "pix",
        scatter_dimension=0,
        tiled=True,
    ).astype(jnp.float32)
    back_q, back_k, back_v = (
        lax.all_gather(query_weight, "pix", axis=0, tiled=True),
        lax.all_gather(key_weight, "pix", axis=0, tiled=True),
        lax.all_gather(value_weight, "pix", axis=0, tiled=True),
    )
    dinput = (
        contract_last(dquery, back_q) + contract_last(dkey, back_k) + contract_last(dvalue, back_v)
    )
    weight_grads = lax.psum(grads, "rep")
    return (dinput.astype(jnp.bfloat16).reshape(tokens.shape), weight_grads)


def solution(mesh):
    placed = (
        P(("pix", "rep"), None, None),
        P(("pix", "rep"), None, None),
        P("pix", None),
        P("pix", None),
        P("pix", None),
        P("pix", None),
    )
    return jax.shard_map(
        local,
        mesh=mesh,
        in_specs=placed,
        out_specs=(P(("pix", "rep"), None, None), P("pix", None)),
        check_vma=False,
    )
```

profile of v0, /device:TPU:0, one launch (start us, length us, event | category | flops | bytes accessed | tf_op | source)
XLA Modules:
  0.0 441.2 jit_solution(11428805849281007432)
XLA Ops:
  10.0 46.1 %all-gather.9.cloned.1.call-done = bf16[1152,1152]{1,0:T(8,128)(2,1)} async-done(((bf16[72,1152]{1,0:T(8,128)(2,1)}), bf16[1152,1152]{1,0:T(8,128)(2,1)}) %all-gather.9.cloned.1.call-update) | async-done | bytes 2654224 | tf_op jit(solution)/shard_map/all_gather | solution.py:51
  56.1 2.8 convolution_convert_fusion.5
  59.8 40.5 %all-gather.11.cloned.1.call-done = bf16[1152,1152]{1,0:T(8,128)(2,1)} async-done(((bf16[72,1152]{1,0:T(8,128)(2,1)}), bf16[1152,1152]{1,0:T(8,128)(2,1)}) %all-gather.11.cloned.1.call-update) | async-done | bytes 2654224 | tf_op jit(solution)/shard_map/all_gather | solution.py:32
  100.3 2.3 convolution_convert_fusion.4
  102.6 0.9 reshape.44
  103.6 40.9 %all-gather.5.cloned.1.call-done = bf16[1152,1152]{1,0:T(8,128)(2,1)} async-done(((bf16[72,1152]{1,0:T(8,128)(2,1)}), bf16[1152,1152]{1,0:T(8,128)(2,1)}) %all-gather.5.cloned.1.call-update) | async-done | bytes 2654224 | tf_op jit(solution)/shard_map/all_gather | solution.py:31
  144.5 2.3 convolution_convert_fusion.7
  147.8 40.8 %all-gather.7.cloned.1.call-done = bf16[1152,1152]{1,0:T(8,128)(2,1)} async-done(((bf16[72,1152]{1,0:T(8,128)(2,1)}), bf16[1152,1152]{1,0:T(8,128)(2,1)}) %all-gather.7.cloned.1.call-update) | async-done | bytes 2654224 | tf_op jit(solution)/shard_map/all_gather | solution.py:30
  188.6 2.3 convolution_convert_fusion.6
  190.9 0.9 reshape.41
  192.3 1.7 fusion.48
  194.0 2.3 fusion.14
  196.3 2.3 fusion.13
  198.6 3.0 fusion.12
  201.6 1.6 fusion.15
  209.7 28.0 %pad_maximum_fusion = bf16[1152,4608]{0,1:T(8,128)(2,1)} fusion(bf16[1152,1152]{0,1:T(8,128)(2,1)S(1)} %convolution_convert_fusion, bf16[1152,1152]{0,1:T(8,128)(2,1)S(1)} %fusion.4, bf16[1152,1152]{0,1:T(8,128)(2,1)S(1)} %fusion.3, bf16[1152,1152]{0,1:T(8,128)(2,1)S(1)} %fusion.2), kind=kLoop, calls=%fused_computation.2 | loop fusion | flops 42467328 | bytes 21233664 | tf_op jit(solution)/shard_map/concatenate | solution.py:74
  237.7 15.3 %copy.51 = bf16[1152,4608]{1,0:T(8,128)(2,1)} copy(bf16[1152,4608]{0,1:T(8,128)(2,1)} %pad_maximum_fusion) | data formatting | bytes 21233664
  253.0 1.7 copy-done.2
  257.4 1.2 copy-done.3
  258.7 1.6 fusion.5
  260.3 112.4 %reduce-scatter.4.cloned.1.call-done = bf16[72,4608]{1,0:T(8,128)(2,1)} async-done(((bf16[1152,4608]{1,0:T(8,128)(2,1)}), bf16[72,4608]{1,0:T(8,128)(2,1)}) %reduce-scatter.4.cloned.1.call-update) | async-done | bytes 663568
  372.7 2.3 copy.52
  375.0 57.9 %all-reduce.1 = f32[72,4608]{0,1:T(8,128)S(1)} all-reduce(bf16[72,4608]{0,1:T(8,128)(2,1)} %copy.52), channel_id=1, replica_groups=mesh['pix'=16,'rep'=2] {'rep'}, use_global_device_ids=true, to_apply=%region_4.0 | all-reduce | flops 331776 | bytes 1990656 | tf_op jit(solution)/shard_map/psum | solution.py:100
  432.9 1.7 copy.48
  (45 shorter events, 13.9 us)
Async XLA Ops:
  7.2 93.1 %copy-start = (bf16[8,16,1152]{2,1,0:T(8,128)(2,1)S(1)}, bf16[8,16,1152]{2,1,0:T(8,128)(2,1)}, u32[]{:S(2)}) copy-start(bf16[8,16,1152]{2,1,0:T(8,128)(2,1)} %param.6) | copy-start | bytes 884740
  7.2 48.9 %all-gather.9.cloned.1.call-start = ((), (), s32[]{:S(2)}) async-start(), calls=%async_computation.3 | async-start | bytes 2820096 | tf_op jit(solution)/shard_map/all_gather | solution.py:51
  7.9 92.4 %all-gather.11.cloned.1.call-start = ((), (), s32[]{:S(2)}) async-start(), calls=%async_computation.4 | async-start | bytes 2820096 | tf_op jit(solution)/shard_map/all_gather | solution.py:32
  8.7 135.8 %all-gather.5.cloned.1.call-start = ((), (), s32[]{:S(2)}) async-start(), calls=%async_computation.1 | async-start | bytes 2820096 | tf_op jit(solution)/shard_map/all_gather | solution.py:31
  9.4 179.2 %all-gather.7.cloned.1.call-start = ((), (), s32[]{:S(2)}) async-start(), calls=%async_computation.2 | async-start | bytes 2820096 | tf_op jit(solution)/shard_map/all_gather | solution.py:30
  10.0 362.7 %reduce-scatter.4.cloned.1.call-start = ((), (), s32[]{:S(2)}) async-start(), calls=%async_computation.5 | async-start | bytes 11280384
  191.9 2.1 copy-start.9
  201.6 1.7 copy-start.8
  203.3 1.3 copy-start.7
  203.9 2.0 copy-start.4
  206.8 1.8 copy-start.6
  253.0 1.7 copy-start.2
  254.7 1.7 copy-start.1
  256.5 2.2 copy-start.3
  256.5 2.2 copy-start.5
Sparse Core Ops, SparseCore 0:
  10.1 45.8 all-gather.8
  58.2 42.0 all-gather.10
  102.4 42.0 all-gather.4
  146.5 42.0 all-gather.6
  253.1 119.5 reduce-scatter.3
where the time goes:
time: 442 us; the launch traced here: 441 us
  waiting for transfers between devices  283 us (64%)
  blocking collectives  57.9 us (13%)
  local copies, waits for them, and re-layouts  29.5 us (7%)
  matrix products  28.1 us (6%)
  other arithmetic  28 us (6%)
  between operations  14.2 us (3%)
    unnamed x6, waiting for transfers between devices  115 us
    psum x1, blocking collectives, local(): weight_grads = lax.psum(grads, 'rep')  57.9 us
    all_gather x1, waiting for transfers between devices, local(): output_full = lax.all_gather(output_weight, 'pix', axis=0, tiled=True)  46.1 us
    all_gather x1, waiting for transfers between devices, local(): lax.all_gather(key_weight, 'pix', axis=0, tiled=True)  40.9 us
    all_gather x1, waiting for transfers between devices, local(): lax.all_gather(query_weight, 'pix', axis=0, tiled=True)  40.8 us
    all_gather x1, waiting for transfers between devices, local(): lax.all_gather(value_weight, 'pix', axis=0, tiled=True)  40.5 us
    concatenate x1, other arithmetic, local(): jnp.concatenate([jnp.concatenate([contract_first(rows, dquery), contract_...  28 us
    unnamed x23, local copies, waits for them, and re-layouts  23.2 us
  transfers between devices with their start and end apart: 5, of which 5 were waited for; matrix products, arithmetic and copies ran while one was open for 3% of the time, Pallas kernels for 0%

commit v1 on v0

--- a/solution.py
+++ b/solution.py
@@ -2,6 +2,7 @@
 import jax.numpy as jnp
 from jax import lax
 from jax.sharding import PartitionSpec as P
+from jax.lax import all_gather
 
 D = 1152
 HEADS = 16
@@ -22,6 +23,11 @@
 
 
 def local(tokens, out_grad, query_weight, key_weight, value_weight, output_weight):
+
+    def matrix_supply_all(here_x):
+        u1 = all_gather(here_x, "rep")
+        return jnp.sum(u1, axis=0)
+
     count = tokens.shape[0]
     rows = tokens.reshape(-1, D)
     drows = out_grad.reshape(-1, D)
@@ -97,7 +103,7 @@
     dinput = (
         contract_last(dquery, back_q) + contract_last(dkey, back_k) + contract_last(dvalue, back_v)
     )
-    weight_grads = lax.psum(grads, "rep")
+    weight_grads = matrix_supply_all(grads)
     return (dinput.astype(jnp.bfloat16).reshape(tokens.shape), weight_grads)
 
 

time: 442 us -> 425 us (0.962)
  blocking collectives: 57.9 us -> 0 us
  waiting for transfers between devices: 283 us -> 323 us
  local copies, waits for them, and re-layouts: 29.5 us -> 22.5 us
  other arithmetic: 28 us -> 33.3 us
    reduce_scatter x0 -> x1, waiting for transfers between devices: none -> 120 us  [local(): lax.psum_scatter(jnp.concatenate([jnp.concatenate([contract_first(rows, d...]
    unnamed x6, waiting for transfers between devices: 115 us -> 2.61 us
    psum x1 -> x0, blocking collectives: 57.9 us -> none  [local(): weight_grads = lax.psum(grads, 'rep')]
    all_gather x0 -> x1, waiting for transfers between devices: none -> 32.9 us  [matrix_supply_all(): u1 = all_gather(here_x, 'rep')]
    unnamed x23 -> x19, local copies, waits for them, and re-layouts: 23.2 us -> 16.1 us
  transfers between devices with their start and end apart: 5 -> 6, of which waited for: 5 -> 6; matrix products, arithmetic and copies ran while one was open for 3% -> 4% of each run, Pallas kernels for 0% -> 0%
where the time goes in v1:
time: 425 us; the launch traced here: 424 us
  waiting for transfers between devices  323 us (76%)
  other arithmetic  33.3 us (8%)
  matrix products  30.2 us (7%)
  local copies, waits for them, and re-layouts  22.5 us (5%)
  between operations  14.5 us (3%)
    reduce_scatter x1, waiting for transfers between devices, local(): lax.psum_scatter(jnp.concatenate([jnp.concatenate([contract_first(rows, d...  120 us
    all_gather x1, waiting for transfers between devices, local(): output_full = lax.all_gather(output_weight, 'pix', axis=0, tiled=True)  46.1 us
    all_gather x1, waiting for transfers between devices, local(): lax.all_gather(key_weight, 'pix', axis=0, tiled=True)  40.9 us
    all_gather x1, waiting for transfers between devices, local(): lax.all_gather(query_weight, 'pix', axis=0, tiled=True)  40.8 us
    all_gather x1, waiting for transfers between devices, local(): lax.all_gather(value_weight, 'pix', axis=0, tiled=True)  40.5 us
    all_gather x1, waiting for transfers between devices, matrix_supply_all(): u1 = all_gather(here_x, 'rep')  32.9 us
    concatenate x1, other arithmetic, local(): jnp.concatenate([jnp.concatenate([contract_first(rows, dquery), contract_...  28 us
    unnamed x19, local copies, waits for them, and re-layouts  16.1 us
  transfers between devices with their start and end apart: 6, of which 6 were waited for; matrix products, arithmetic and copies ran while one was open for 4% of the time, Pallas kernels for 0%

profile of v1, /device:TPU:0, one launch (start us, length us, event | category | flops | bytes accessed | tf_op | source)
XLA Modules:
  0.0 424.2 jit_solution(10470038934049325147)
XLA Ops:
  10.0 46.1 %all-gather.11.cloned.1.call-done = bf16[1152,1152]{1,0:T(8,128)(2,1)} async-done(((bf16[72,1152]{1,0:T(8,128)(2,1)}), bf16[1152,1152]{1,0:T(8,128)(2,1)}) %all-gather.11.cloned.1.call-update) | async-done | bytes 2654224 | tf_op jit(solution)/shard_map/all_gather | solution.py:57
  56.1 2.8 convolution_convert_fusion.5
  58.9 0.9 reshape.43
  59.8 40.5 %all-gather.13.cloned.1.call-done = bf16[1152,1152]{1,0:T(8,128)(2,1)} async-done(((bf16[72,1152]{1,0:T(8,128)(2,1)}), bf16[1152,1152]{1,0:T(8,128)(2,1)}) %all-gather.13.cloned.1.call-update) | async-done | bytes 2654224 | tf_op jit(solution)/shard_map/all_gather | solution.py:38
  100.3 2.3 convolution_convert_fusion.4
  102.6 0.9 reshape.44
  103.6 40.9 %all-gather.7.cloned.1.call-done = bf16[1152,1152]{1,0:T(8,128)(2,1)} async-done(((bf16[72,1152]{1,0:T(8,128)(2,1)}), bf16[1152,1152]{1,0:T(8,128)(2,1)}) %all-gather.7.cloned.1.call-update) | async-done | bytes 2654224 | tf_op jit(solution)/shard_map/all_gather | solution.py:37
  144.5 2.3 convolution_convert_fusion.7
  147.8 40.8 %all-gather.9.cloned.1.call-done = bf16[1152,1152]{1,0:T(8,128)(2,1)} async-done(((bf16[72,1152]{1,0:T(8,128)(2,1)}), bf16[1152,1152]{1,0:T(8,128)(2,1)}) %all-gather.9.cloned.1.call-update) | async-done | bytes 2654224 | tf_op jit(solution)/shard_map/all_gather | solution.py:36
  188.6 2.3 convolution_convert_fusion.6
  190.9 0.9 reshape.41
  192.3 1.7 fusion.48
  194.0 2.3 fusion.14
  196.3 2.3 fusion.13
  198.6 3.2 fusion.12
  201.7 1.6 fusion.15
  209.8 28.0 %pad_maximum_fusion = bf16[1152,4608]{0,1:T(8,128)(2,1)} fusion(bf16[1152,1152]{0,1:T(8,128)(2,1)S(1)} %convolution_convert_fusion, bf16[1152,1152]{0,1:T(8,128)(2,1)S(1)} %fusion.4, bf16[1152,1152]{0,1:T(8,128)(2,1)S(1)} %fusion.3, bf16[1152,1152]{0,1:T(8,128)(2,1)S(1)} %fusion.2), kind=kLoop, calls=%fused_computation.2 | loop fusion | flops 42467328 | bytes 21233664 | tf_op jit(solution)/shard_map/concatenate | solution.py:80
  237.8 15.3 %copy.65 = bf16[1152,4608]{1,0:T(8,128)(2,1)} copy(bf16[1152,4608]{0,1:T(8,128)(2,1)} %pad_maximum_fusion) | data formatting | bytes 21233664
  253.1 119.6 %reduce-scatter.4.cloned.1.call-done = bf16[72,4608]{1,0:T(8,128)(2,1)} async-done(((bf16[1152,4608]{1,0:T(8,128)(2,1)}), bf16[72,4608]{1,0:T(8,128)(2,1)}) %reduce-scatter.4.cloned.1.call-update) | async-done | bytes 663568 | tf_op jit(solution)/shard_map/reduce_scatter | solution.py:79
  372.7 2.3 all_gather.31
  375.0 2.8 fusion.53
  379.6 1.6 fusion.5
  381.2 32.9 %all-gather.15.cloned.1.call-done = f32[144,4608]{1,0:T(8,128)} async-done(((f32[72,4608]{1,0:T(8,128)}), f32[144,4608]{1,0:T(8,128)}) %all-gather.15.cloned.1.call-update) | async-done | bytes 2654224 | tf_op jit(solution)/shard_map/all_gather | solution.py:28
  414.2 3.1 reduce_sum.29
  (45 shorter events, 12.1 us)
Async XLA Ops:
  7.2 93.1 %copy-start = (bf16[8,16,1152]{2,1,0:T(8,128)(2,1)S(1)}, bf16[8,16,1152]{2,1,0:T(8,128)(2,1)}, u32[]{:S(2)}) copy-start(bf16[8,16,1152]{2,1,0:T(8,128)(2,1)} %param.6) | copy-start | bytes 884740
  7.2 48.9 %all-gather.11.cloned.1.call-start = ((), (), s32[]{:S(2)}) async-start(), calls=%async_computation.3 | async-start | bytes 2820096 | tf_op jit(solution)/shard_map/all_gather | solution.py:57
  7.9 92.4 %all-gather.13.cloned.1.call-start = ((), (), s32[]{:S(2)}) async-start(), calls=%async_computation.4 | async-start | bytes 2820096 | tf_op jit(solution)/shard_map/all_gather | solution.py:38
  8.7 135.8 %all-gather.7.cloned.1.call-start = ((), (), s32[]{:S(2)}) async-start(), calls=%async_computation.1 | async-start | bytes 2820096 | tf_op jit(solution)/shard_map/all_gather | solution.py:37
  9.4 179.2 %all-gather.9.cloned.1.call-start = ((), (), s32[]{:S(2)}) async-start(), calls=%async_computation.2 | async-start | bytes 2820096 | tf_op jit(solution)/shard_map/all_gather | solution.py:36
  10.0 362.8 %reduce-scatter.4.cloned.1.call-start = ((), (), s32[]{:S(2)}) async-start(), calls=%async_computation.6 | async-start | bytes 11280384 | tf_op jit(solution)/shard_map/reduce_scatter | solution.py:79
  191.9 2.1 copy-start.8
  201.7 1.6 copy-start.7
  203.4 1.3 copy-start.6
  204.1 2.0 copy-start.3
  206.9 1.8 copy-start.5
  253.1 161.1 %all-gather.15.cloned.1.call-start = ((), (), s32[]{:S(2)}) async-start(), calls=%async_computation.5 | async-start | bytes 3981312 | tf_op jit(solution)/shard_map/all_gather | solution.py:28
  375.0 2.8 copy-start.1
  377.9 1.8 copy-start.2
  377.9 1.8 copy-start.4
Sparse Core Ops, SparseCore 0:
  10.1 45.8 all-gather.10
  58.2 42.0 all-gather.12
  102.4 42.0 all-gather.6
  146.5 42.0 all-gather.8
  253.2 119.5 reduce-scatter.3
  375.1 38.9 all-gather.14
